TPU v7x, 256 devices: a whole 4x4x8 slice. The times are simulated.
256 devices in a mesh: gx: 32 (over y, z), gy: 8 (over x, core).
Axes of the slice: x: 4, y: 4, z: 8, core: 2. Of those that a mesh axis runs over, the one named last changes fastest.
Arguments:
- normed: bfloat16 [163840, 1024], P(('gx', 'gy')), may hold values from -6 to 6
- grad_query: bfloat16 [163840, 1024], P(('gx', 'gy')), may hold values from -0.25 to 0.25
- grad_key: bfloat16 [163840, 1024], P(('gx', 'gy')), may hold values from -0.25 to 0.25
- error: bfloat16 [512, 1024, 1024], P(('gx', 'gy')), may hold values from -8 to 8
- start_factor: float32 [2, 32, 1024], replicated, may hold values from -6 to 6
Outputs:
- new_error: bfloat16 [512, 1024, 1024], P(('gx', 'gy'))
- left_factor: float32 [2, 32, 1024], replicated
- right_factor: float32 [2, 32, 1024], replicated
All inputs are finite; a program needn't handle non-finite values.
Results may differ from a plain program's by a relative error of at most 0.001.
Values sent between devices are 32-bit elements; how exact they have to be, the bound alone decides.
A program may use at most 64 MiB of HBM per device.

v0:
```python
import jax
import jax.numpy as jnp
from jax import lax
from jax.sharding import PartitionSpec as P

HIGHEST = lax.Precision.HIGHEST
CONTRACT = (((0,), (0,)), ((), ()))


def gram_of(factor_rows):
    return jnp.einsum("bki,bli->bkl", factor_rows, factor_rows, precision=HIGHEST)


def solve_rows(gram_matrix, factor_rows):
    width = gram_matrix.shape[-1]
    identity = jnp.eye(width, dtype=jnp.float32)
    trace_value = jnp.trace(gram_matrix, axis1=1, axis2=2)
    shift_value = 1e-06 * (trace_value / width + 1.0)
    lower_factor = jnp.linalg.cholesky(gram_matrix + shift_value[:, None, None] * identity)
    return lax.linalg.triangular_solve(lower_factor, factor_rows, left_side=True, lower=True)


def local_left(merged, start_rows):
    return jnp.einsum("bkj,bij->bki", start_rows, merged, precision=HIGHEST)


def local_right(left_rows, merged):
    return jnp.einsum("bki,bij->bkj", left_rows, merged, precision=HIGHEST)


def single_factors(merged, start_rows, replicas):
    left_total = lax.psum(local_left(merged, start_rows), ("gx", "gy"))
    left_rows = solve_rows(gram_of(left_total), left_total)
    right_total = lax.psum(local_right(left_rows, merged), ("gx", "gy"))
    return (left_rows, right_total / replicas)


def on_device(normed, grad_query, grad_key, error, start_factor):
    replicas = lax.axis_size("gx") * lax.axis_size("gy")
    query_grad = lax.dot_general(normed, grad_query, CONTRACT, preferred_element_type=jnp.float32)
    query_merged = query_grad + error[0].astype(jnp.float32)
    query_left, query_right = single_factors(query_merged[None], start_factor[0:1], replicas)
    key_grad = lax.dot_general(normed, grad_key, CONTRACT, preferred_element_type=jnp.float32)
    key_merged = key_grad + error[1].astype(jnp.float32)
    key_left, key_right = single_factors(key_merged[None], start_factor[1:2], replicas)
    merged = jnp.stack([query_merged, key_merged])
    left_rows = jnp.concatenate([query_left, key_left], axis=0)
    right_rows = jnp.concatenate([query_right, key_right], axis=0)
    approx = jnp.einsum("bki,bkj->bij", left_rows, right_rows, precision=HIGHEST)
    return ((merged - approx).astype(jnp.bfloat16), left_rows, right_rows)


def solution(mesh):
    placed = (
        P(("gx", "gy"), None),
        P(("gx", "gy"), None),
        P(("gx", "gy"), None),
        P(("gx", "gy"), None, None),
        P(),
    )
    return jax.shard_map(
        on_device,
        mesh=mesh,
        in_specs=placed,
        out_specs=(P(("gx", "gy"), None, None), P(), P()),
        check_vma=False,
    )
```

profile of v0, /device:TPU:2, one launch (start us, length us, event | category | flops | bytes accessed | tf_op | source)
XLA Modules:
  0.0 575.3 jit_solution(298892361489647621)
XLA Ops:
  7.2 0.0 copy-start
  7.2 0.0 copy-start.8
  7.2 0.0 all-reduce.7.cloned.1.call-start
  7.2 1.3 copy-done
  8.5 0.0 copy-start.7
  8.5 4.0 convert_add_fusion.1
  12.5 0.0 copy-done.8
  12.5 0.0 copy-done.7
  12.5 0.0 copy-start.1
  12.5 0.0 copy-start.6
  12.5 1.8 convert_add_fusion
  14.4 0.1 copy-done.1
  14.5 0.0 copy-done.6
  14.5 0.0 copy-start.2
  14.5 4.6 convolution_bitcast_fusion.3
  19.1 0.0 copy-done.2
  19.1 4.6 convolution_bitcast_fusion.2
  23.6 0.0 all-reduce.7.cloned.1.call-update
  23.7 0.2 all-reduce.5.cloned.1.call-start
  23.9 253.5 %all-reduce.7.cloned.1.call-done = (f32[1,32,1024]{2,1,0:T(8,128)}, f32[1,32,1024]{2,1,0:T(8,128)}) async-done(((f32[1,32,1024]{2,1,0:T(8,128)}, f32[1,32,1024]{2,1,0:T(8,128)}), (f32[1,32,1024]{2,1,0:T(8,128)}, f32[1,32,1024]{2,1,0:T(8,128)})) %all-reduce.7.cloned.1.call-update) | async-done | bytes 262160 | tf_op jit(solution)/shard_map/psum | solution.py:32
  277.4 1.8 select_reduce_fusion.2
  279.9 0.1 copy.13
  280.0 2.9 custom-call.10
  282.9 0.6 compare_reduce_fusion
  283.6 0.7 fusion.14
  284.2 2.4 custom-call.11
  286.7 1.2 fusion.1
  287.9 1.8 select_reduce_fusion.3
  290.4 0.1 copy.10
  290.5 2.9 custom-call.8
  293.5 0.6 compare_reduce_fusion.1
  294.1 0.7 fusion.13
  294.8 2.4 custom-call.9
  297.2 0.0 copy-start.3
  297.2 1.4 fusion.6
  298.6 5.3 convolution_bitcast_fusion.1
  304.0 0.0 copy-done.3
  304.0 3.1 convolution_bitcast_fusion
  307.1 0.0 all-reduce.5.cloned.1.call-update
  307.2 0.0 copy-start.4
  307.2 249.5 %all-reduce.5.cloned.1.call-done = (f32[1,32,1024]{2,1,0:T(8,128)}, f32[1,32,1024]{2,1,0:T(8,128)}) async-done(((f32[1,32,1024]{2,1,0:T(8,128)}, f32[1,32,1024]{2,1,0:T(8,128)}), (f32[1,32,1024]{2,1,0:T(8,128)}, f32[1,32,1024]{2,1,0:T(8,128)})) %all-reduce.5.cloned.1.call-update) | async-done | bytes 262160 | tf_op jit(solution)/shard_map/psum | solution.py:34
  556.7 1.0 broadcast_multiply_fusion
  557.7 0.0 copy-start.5
  557.7 10.7 %fusion = bf16[2,1024,1024]{2,1,0:T(8,128)(2,1)} fusion(f32[1,1024,1024]{2,1,0:T(8,128)} %bitcast.81, f32[1,1024,1024]{2,1,0:T(8,128)} %bitcast.80, f32[2,32,1024]{2,1,0:T(8,128)S(1)} %pad_maximum_fusion, f32[2,32,1024]{2,1,0:T(8,128)S(1)} %pad_maximum_fusion.1), kind=kOutput, calls=%fused_computation.1 | convolution fusion | flops 811597824 | bytes 13107200 | tf_op jit(solution)/shard_map/bki,bkj->bij/dot_general | solution.py:49
  568.4 0.0 copy-done.4
  568.4 0.0 copy-done.5
  (8 shorter events, 0.1 us)
Async XLA Ops:
  7.2 1.3 copy-start
  7.2 5.3 copy-start.8
  7.2 270.2 %all-reduce.7.cloned.1.call-start = ((), (), s32[]{:S(2)}) async-start(), calls=%async_computation.1 | async-start | bytes 524288 | tf_op jit(solution)/shard_map/psum | solution.py:32
  8.5 4.0 copy-start.7
  12.5 2.0 copy-start.1
  12.5 2.0 copy-start.6
  14.5 4.6 copy-start.2
  23.7 533.0 %all-reduce.5.cloned.1.call-start = ((), (), s32[]{:S(2)}) async-start(), calls=%async_computation | async-start | bytes 524288 | tf_op jit(solution)/shard_map/psum | solution.py:34
  297.2 6.7 %copy-start.3 = (f32[1024,1024]{1,0:T(8,128)S(1)}, f32[1024,1024]{1,0:T(8,128)}, u32[]{:S(2)}) copy-start(f32[1024,1024]{1,0:T(8,128)} %copy-done.2) | copy-start | bytes 12582916
  307.2 261.3 %copy-start.4 = (f32[2,32,1024]{2,1,0:T(8,128)}, f32[2,32,1024]{2,1,0:T(8,128)S(1)}, u32[]{:S(2)}) copy-start(f32[2,32,1024]{2,1,0:T(8,128)S(1)} %pad_maximum_fusion) | copy-start | bytes 786436
  557.7 10.7 %copy-start.5 = (f32[2,32,1024]{2,1,0:T(8,128)}, f32[2,32,1024]{2,1,0:T(8,128)S(1)}, u32[]{:S(2)}) copy-start(f32[2,32,1024]{2,1,0:T(8,128)S(1)} %pad_maximum_fusion.1) | copy-start | bytes 786436
Sparse Core Ops, SparseCore 0:
  23.8 253.5 all-reduce.6
  307.2 249.3 all-reduce.4
where the time goes:
time: 576 us; the launch traced here: 575 us
  waiting for transfers between devices  503 us (87%)
  matrix products  40.5 us (7%)
  between operations  15.5 us (3%)
  other arithmetic  14.4 us (2%)
    psum x1, waiting for transfers between devices, single_factors(): left_total = lax.psum(local_left(merged, start_rows), ('gx', 'gy'))  254 us
    psum x1, waiting for transfers between devices, single_factors(): right_total = lax.psum(local_right(left_rows, merged), ('gx', 'gy'))  250 us
  transfers between devices with their start and end apart: 2, of which 2 were waited for; matrix products, arithmetic and copies ran while one was open for 0% of the time, Pallas kernels for 0%

commit v1 on v0

--- a/solution.py
+++ b/solution.py
@@ -29,7 +29,7 @@
 
 
 def single_factors(merged, start_rows, replicas):
-    left_total = lax.psum(local_left(merged, start_rows), ("gx", "gy"))
+    left_total = lax.psum(lax.psum(local_left(merged, start_rows), "gx"), "gy")
     left_rows = solve_rows(gram_of(left_total), left_total)
     right_total = lax.psum(local_right(left_rows, merged), ("gx", "gy"))
     return (left_rows, right_total / replicas)

time: 576 us -> 534 us (0.927)
  waiting for transfers between devices: 503 us -> 461 us
    psum x1 -> x2, waiting for transfers between devices: 254 us -> 209 us  [single_factors(): left_total = lax.psum(lax.psum(local_left(merged, start_rows), 'gx'), 'gy')]
  transfers between devices with their start and end apart: 2 -> 3, of which waited for: 2 -> 3; matrix products, arithmetic and copies ran while one was open for 0% -> 0% of each run, Pallas kernels for 0% -> 0%
where the time goes in v1:
time: 534 us; the launch traced here: 533 us
  waiting for transfers between devices  461 us (86%)
  matrix products  40.5 us (8%)
  between operations  15.2 us (3%)
  other arithmetic  14.4 us (3%)
    psum x1, waiting for transfers between devices, single_factors(): right_total = lax.psum(local_right(left_rows, merged), ('gx', 'gy'))  252 us
    psum x2, waiting for transfers between devices, single_factors(): left_total = lax.psum(lax.psum(local_left(merged, start_rows), 'gx'), 'gy')  209 us
    dot_general x1, matrix products, on_device(): jnp.einsum('bki,bkj->bij', left_rows, right_rows, precision=HIGHEST)  10.7 us
  transfers between devices with their start and end apart: 3, of which 3 were waited for; matrix products, arithmetic and copies ran while one was open for 0% of the time, Pallas kernels for 0%

profile of v1, /device:TPU:2, one launch (start us, length us, event | category | flops | bytes accessed | tf_op | source)
XLA Modules:
  0.0 533.4 jit_solution(15978668341715493654)
XLA Ops:
  7.2 0.0 copy-start
  7.2 0.0 copy-start.8
  7.2 0.0 all-reduce.9.cloned.1.call-start
  7.2 1.3 copy-done
  8.5 0.0 copy-start.7
  8.5 4.0 convert_add_fusion.1
  12.5 0.0 copy-done.8
  12.5 0.0 copy-done.7
  12.5 0.0 copy-start.1
  12.5 0.0 copy-start.6
  12.5 1.8 convert_add_fusion
  14.4 0.1 copy-done.1
  14.5 0.0 copy-done.6
  14.5 0.0 copy-start.2
  14.5 4.6 convolution_bitcast_fusion.3
  19.1 0.0 copy-done.2
  19.1 4.6 convolution_bitcast_fusion.2
  23.6 0.0 all-reduce.9.cloned.1.call-update
  23.7 0.0 all-reduce.11.cloned.1.call-start
  23.7 147.3 %all-reduce.9.cloned.1.call-done = (f32[1,32,1024]{2,1,0:T(8,128)}, f32[1,32,1024]{2,1,0:T(8,128)}) async-done(((f32[1,32,1024]{2,1,0:T(8,128)}, f32[1,32,1024]{2,1,0:T(8,128)}), (f32[1,32,1024]{2,1,0:T(8,128)}, f32[1,32,1024]{2,1,0:T(8,128)})) %all-reduce.9.cloned.1.call-update) | async-done | bytes 262160 | tf_op jit(solution)/shard_map/psum | solution.py:32
  171.0 0.0 all-reduce.11.cloned.1.call-update
  171.0 0.2 all-reduce.7.cloned.1.call-start
  171.3 62.0 %all-reduce.11.cloned.1.call-done = (f32[1,32,1024]{2,1,0:T(8,128)}, f32[1,32,1024]{2,1,0:T(8,128)}) async-done(((f32[1,32,1024]{2,1,0:T(8,128)}, f32[1,32,1024]{2,1,0:T(8,128)}), (f32[1,32,1024]{2,1,0:T(8,128)}, f32[1,32,1024]{2,1,0:T(8,128)})) %all-reduce.11.cloned.1.call-update) | async-done | bytes 262160 | tf_op jit(solution)/shard_map/psum | solution.py:32
  233.3 1.8 select_reduce_fusion.2
  235.8 0.1 copy.13
  235.9 2.9 custom-call.10
  238.8 0.6 compare_reduce_fusion
  239.5 0.7 fusion.14
  240.1 2.4 custom-call.11
  242.6 1.2 fusion.1
  243.8 1.8 select_reduce_fusion.3
  246.3 0.1 copy.10
  246.4 2.9 custom-call.8
  249.3 0.6 compare_reduce_fusion.1
  250.0 0.7 fusion.13
  250.6 2.4 custom-call.9
  253.1 1.4 fusion.6
  254.5 5.3 convolution_bitcast_fusion.1
  259.8 0.0 copy-done.3
  259.8 3.1 convolution_bitcast_fusion
  263.0 0.0 all-reduce.7.cloned.1.call-update
  263.0 0.0 copy-start.4
  263.0 252.1 %all-reduce.7.cloned.1.call-done = (f32[1,32,1024]{2,1,0:T(8,128)}, f32[1,32,1024]{2,1,0:T(8,128)}) async-done(((f32[1,32,1024]{2,1,0:T(8,128)}, f32[1,32,1024]{2,1,0:T(8,128)}), (f32[1,32,1024]{2,1,0:T(8,128)}, f32[1,32,1024]{2,1,0:T(8,128)})) %all-reduce.7.cloned.1.call-update) | async-done | bytes 262160 | tf_op jit(solution)/shard_map/psum | solution.py:34
  515.1 1.0 broadcast_multiply_fusion
  516.1 0.0 copy-start.5
  516.1 10.7 %fusion = bf16[2,1024,1024]{2,1,0:T(8,128)(2,1)} fusion(f32[1,1024,1024]{2,1,0:T(8,128)} %bitcast.81, f32[1,1024,1024]{2,1,0:T(8,128)} %bitcast.80, f32[2,32,1024]{2,1,0:T(8,128)S(1)} %pad_maximum_fusion, f32[2,32,1024]{2,1,0:T(8,128)S(1)} %pad_maximum_fusion.1), kind=kOutput, calls=%fused_computation.1 | convolution fusion | flops 811597824 | bytes 13107200 | tf_op jit(solution)/shard_map/bki,bkj->bij/dot_general | solution.py:49
  526.9 0.0 copy-done.4
  526.9 0.0 copy-done.5
  (9 shorter events, 0.1 us)
Async XLA Ops:
  7.2 1.3 copy-start
  7.2 5.3 copy-start.8
  7.2 163.8 %all-reduce.9.cloned.1.call-start = ((), (), s32[]{:S(2)}) async-start(), calls=%async_computation.1 | async-start | bytes 524288 | tf_op jit(solution)/shard_map/psum | solution.py:32
  8.5 4.0 copy-start.7
  12.5 2.0 copy-start.1
  12.5 2.0 copy-start.6
  14.5 4.6 copy-start.2
  23.7 209.6 %all-reduce.11.cloned.1.call-start = ((), (), s32[]{:S(2)}) async-start(), calls=%async_computation.2 | async-start | bytes 524288 | tf_op jit(solution)/shard_map/psum | solution.py:32
  171.0 344.1 %all-reduce.7.cloned.1.call-start = ((), (), s32[]{:S(2)}) async-start(), calls=%async_computation | async-start | bytes 524288 | tf_op jit(solution)/shard_map/psum | solution.py:34
  253.1 6.7 %copy-start.3 = (f32[1024,1024]{1,0:T(8,128)S(1)}, f32[1024,1024]{1,0:T(8,128)}, u32[]{:S(2)}) copy-start(f32[1024,1024]{1,0:T(8,128)} %copy-done.2) | copy-start | bytes 12582916
  263.0 263.8 %copy-start.4 = (f32[2,32,1024]{2,1,0:T(8,128)}, f32[2,32,1024]{2,1,0:T(8,128)S(1)}, u32[]{:S(2)}) copy-start(f32[2,32,1024]{2,1,0:T(8,128)S(1)} %pad_maximum_fusion) | copy-start | bytes 786436
  516.1 10.7 %copy-start.5 = (f32[2,32,1024]{2,1,0:T(8,128)}, f32[2,32,1024]{2,1,0:T(8,128)S(1)}, u32[]{:S(2)}) copy-start(f32[2,32,1024]{2,1,0:T(8,128)S(1)} %pad_maximum_fusion.1) | copy-start | bytes 786436
Sparse Core Ops, SparseCore 0:
  23.8 147.1 all-reduce.8
  173.4 59.8 all-reduce.10
  263.1 251.9 all-reduce.6
